TPU v7x, 256 devices: a whole 4x4x8 slice. The times are simulated.
256 devices in a mesh: heads: 4 (over x), pages: 64 (over z, y, core).
Axes of the slice: x: 4, y: 4, z: 8, core: 2. Of those that a mesh axis runs over, the one named last changes fastest.
Arguments:
- queries: bfloat16 [4608, 16, 128], P('pages', 'heads'), may hold values from -60 to 60
- keys: bfloat16 [4608, 16, 128], P('pages', 'heads'), may hold values from -6 to 6
- values: bfloat16 [4608, 16, 128], P('pages', 'heads'), may hold values from -6 to 6
- key_cache: bfloat16 [768, 128, 16, 128], P('pages', None, 'heads'), may hold values from -6 to 6
- value_cache: bfloat16 [768, 128, 16, 128], P('pages', None, 'heads'), may hold values from -6 to 6
- cache_len: int32 [6], replicated, may hold values from 0 to 15616, as said below
- page_table: int32 [6, 122], replicated, may hold values from 0 to 767, as said below
- append_slots: int32 [6, 6], replicated, may hold values from 0 to 767
- out_weight: bfloat16 [2048, 4096], P('heads', 'pages'), may hold values from -0.125 to 0.125
- out_bias: float32 [4096], P('heads'), may hold values from -3 to 3
Outputs:
- hidden: bfloat16 [4608, 4096], P('pages', 'heads')
- key_cache_out: bfloat16 [768, 128, 16, 128], P('pages', None, 'heads')
- value_cache_out: bfloat16 [768, 128, 16, 128], P('pages', None, 'heads')
Inputs may be any that keep to these rules, and one draw needn't show every extreme that they name: Every entry of page_table and append_slots together is a different slot. `cache_len`: A multiple of 128; some request has exactly 15616.
All inputs are finite; a program needn't handle non-finite values.
Results may differ from a plain program's by a relative error of at most 0.018.
Values may be sent and summed in bfloat16 or wider, within the bound.
A program may use at most 128 MiB of HBM per device.

v0:
```python
import math
import jax
import jax.numpy as jnp
from jax import lax
from jax.sharding import PartitionSpec as P

ROT = 32
PAGE = 128
low_score = -1e30


def rotate(vectors, positions):
    half_rot = ROT // 2
    inv_freq = 10000.0 ** (-2.0 * jnp.arange(half_rot, dtype=jnp.float32) / ROT)
    angles = positions[:, None] * inv_freq[None, :]
    cosine = jnp.cos(angles)[:, None, :]
    sine = jnp.sin(angles)[:, None, :]
    first_half = vectors[..., :half_rot]
    second_half = vectors[..., half_rot:ROT]
    return jnp.concatenate(
        [
            first_half * cosine - second_half * sine,
            second_half * cosine + first_half * sine,
            vectors[..., ROT:],
        ],
        axis=-1,
    )


def per_device(
    queries,
    keys,
    values,
    key_cache,
    value_cache,
    cache_len,
    page_table,
    append_slots,
    out_weight,
    out_bias,
):
    tok_dev, head_count, head_dim = queries.shape
    requests = cache_len.shape[0]
    max_pages = page_table.shape[1]
    new_pages = append_slots.shape[1]
    span_len = new_pages * PAGE
    slot_count = key_cache.shape[0]
    device_at = lax.axis_index("pages")
    token_ids = device_at * tok_dev + jnp.arange(tok_dev, dtype=jnp.int32)
    request_ids = token_ids // span_len
    request_grid = jnp.arange(requests, dtype=jnp.int32)
    starts = jnp.sum(
        jnp.where(request_ids[:, None] == request_grid[None, :], cache_len[None, :], 0), axis=1
    )
    positions = (starts + token_ids % span_len).astype(jnp.float32)
    rotated_q = rotate(queries.astype(jnp.float32), positions).astype(jnp.bfloat16)
    rotated_k = rotate(keys.astype(jnp.float32), positions).astype(jnp.bfloat16)
    all_q, all_k, all_v = (
        lax.all_gather(rotated_q, "pages", axis=0, tiled=True),
        lax.all_gather(rotated_k, "pages", axis=0, tiled=True),
        lax.all_gather(values, "pages", axis=0, tiled=True),
    )
    my_slots = device_at * slot_count + jnp.arange(slot_count, dtype=jnp.int32)
    cached_hit = page_table.reshape(-1)[None, :] == my_slots[:, None]
    fresh_hit = append_slots.reshape(-1)[None, :] == my_slots[:, None]
    is_cached = jnp.any(cached_hit, axis=1)
    is_fresh = jnp.any(fresh_hit, axis=1)
    cached_index = jnp.sum(
        jnp.where(cached_hit, jnp.arange(requests * max_pages, dtype=jnp.int32)[None, :], 0), axis=1
    )
    fresh_index = jnp.sum(
        jnp.where(fresh_hit, jnp.arange(requests * new_pages, dtype=jnp.int32)[None, :], 0), axis=1
    )
    slot_request = jnp.where(is_fresh, fresh_index // new_pages, cached_index // max_pages)
    slot_page = jnp.where(is_fresh, fresh_index % new_pages, cached_index % max_pages)
    slot_length = jnp.sum(
        jnp.where(slot_request[:, None] == request_grid[None, :], cache_len[None, :], 0), axis=1
    )
    page_shape = (requests * new_pages, PAGE, head_count, head_dim)
    key_out = jnp.where(
        is_fresh[:, None, None, None],
        jnp.take(all_k.reshape(page_shape), fresh_index, axis=0),
        key_cache,
    )
    value_out = jnp.where(
        is_fresh[:, None, None, None],
        jnp.take(all_v.reshape(page_shape), fresh_index, axis=0),
        value_cache,
    )
    query_blocks = all_q.reshape(requests, span_len, head_count, head_dim)
    score_scale = 1.0 / math.sqrt(head_dim)
    query_offsets = jnp.arange(span_len, dtype=jnp.int32)
    key_offsets = jnp.arange(PAGE, dtype=jnp.int32)

    def slot_scores(slot):
        request = slot_request[slot]
        query_block = lax.dynamic_index_in_dim(query_blocks, request, 0, keepdims=False)
        key_block = lax.dynamic_index_in_dim(key_out, slot, 0, keepdims=False)
        scores = (
            jnp.einsum("qhd,khd->hqk", query_block, key_block, preferred_element_type=jnp.float32)
            * score_scale
        )
        length = slot_length[slot]
        base_pos = slot_page[slot] * PAGE + key_offsets
        cached_ok = is_cached[slot] & (base_pos < length)
        fresh_ok = is_fresh[slot] & (base_pos[None, :] <= query_offsets[:, None])
        allowed = cached_ok[None, :] | fresh_ok
        return (jnp.where(allowed[None], scores, low_score), request, allowed)

    def over_slots(step, start):
        return lax.fori_loop(0, slot_count, step, start)

    def peak_step(slot, peaks):
        scores, request, allowed = slot_scores(slot)
        local_max = jnp.transpose(jnp.max(scores, axis=2))
        earlier = lax.dynamic_index_in_dim(peaks, request, 0, keepdims=False)
        return lax.dynamic_update_index_in_dim(peaks, jnp.maximum(earlier, local_max), request, 0)

    peaks = over_slots(
        peak_step, jnp.full((requests, span_len, head_count), low_score, jnp.float32)
    )
    peaks = lax.pmax(peaks.astype(jnp.bfloat16), "pages").astype(peaks.dtype)

    def weigh_step(slot, carry):
        weighted, totals = carry
        scores, request, allowed = slot_scores(slot)
        row_peak = jnp.transpose(lax.dynamic_index_in_dim(peaks, request, 0, keepdims=False))
        weights = jnp.exp(scores - row_peak[:, :, None])
        value_block = lax.dynamic_index_in_dim(value_out, slot, 0, keepdims=False)
        contrib = jnp.einsum(
            "hqk,khd->qhd",
            weights.astype(jnp.bfloat16),
            value_block,
            preferred_element_type=jnp.float32,
        )
        earlier = lax.dynamic_index_in_dim(weighted, request, 0, keepdims=False)
        weighted = lax.dynamic_update_index_in_dim(weighted, earlier + contrib, request, 0)
        row_sums = jnp.transpose(jnp.sum(weights, axis=2))
        earlier_sums = lax.dynamic_index_in_dim(totals, request, 0, keepdims=False)
        totals = lax.dynamic_update_index_in_dim(totals, earlier_sums + row_sums, request, 0)
        return (weighted, totals)

    start_sums = (
        jnp.zeros((requests, span_len, head_count, head_dim), jnp.float32),
        jnp.zeros((requests, span_len, head_count), jnp.float32),
    )
    weighted, totals = over_slots(weigh_step, start_sums)
    weighted, totals = (
        lax.psum_scatter(
            weighted.reshape(requests * span_len, head_count * head_dim),
            "pages",
            scatter_dimension=0,
            tiled=True,
        ),
        lax.psum_scatter(
            totals.reshape(requests * span_len, head_count),
            "pages",
            scatter_dimension=0,
            tiled=True,
        ),
    )
    attended = (
        (weighted.reshape(tok_dev, head_count, head_dim) / totals[:, :, None])
        .reshape(tok_dev, head_count * head_dim)
        .astype(jnp.bfloat16)
    )
    projected = jnp.dot(
        attended,
        lax.all_gather(out_weight, "pages", axis=1, tiled=True),
        preferred_element_type=jnp.float32,
    )
    summed = lax.psum_scatter(
        projected.astype(jnp.bfloat16), "heads", scatter_dimension=1, tiled=True
    ).astype(jnp.float32)
    hidden = (summed + out_bias[None, :]).astype(jnp.bfloat16)
    return (hidden, key_out, value_out)


def solution(mesh):
    placed = (
        P("pages", "heads", None),
        P("pages", "heads", None),
        P("pages", "heads", None),
        P("pages", None, "heads", None),
        P("pages", None, "heads", None),
        P(),
        P(),
        P(),
        P("heads", "pages"),
        P("heads"),
    )
    return jax.shard_map(
        per_device,
        mesh=mesh,
        in_specs=placed,
        out_specs=(
            P("pages", "heads"),
            P("pages", None, "heads", None),
            P("pages", None, "heads", None),
        ),
        check_vma=False,
    )
```

profile of v0, /device:TPU:8, one launch (start us, length us, event | category | flops | bytes accessed | tf_op | source)
XLA Modules:
  0.0 1257.5 jit_solution(8616648984599023867)
XLA Ops:
  14.0 78.4 %all-gather.9.cloned.1.call-done = bf16[4608,4,128]{2,0,1:T(8,128)(2,1)} async-done(((bf16[72,4,128]{2,0,1:T(8,128)(2,1)}), bf16[4608,4,128]{2,0,1:T(8,128)(2,1)}) %all-gather.9.cloned.1.call-update) | async-done | bytes 4718608 | tf_op jit(solution)/shard_map/all_gather | solution.py:60
  92.4 6.3 copy.77
  98.7 73.7 %all-gather.5.cloned.1.call-done = bf16[4608,4,128]{2,0,1:T(8,128)(2,1)} async-done(((bf16[72,4,128]{2,0,1:T(8,128)(2,1)}), bf16[4608,4,128]{2,0,1:T(8,128)(2,1)}) %all-gather.5.cloned.1.call-update) | async-done | bytes 4718608 | tf_op jit(solution)/shard_map/all_gather | solution.py:61
  172.4 6.4 copy.71
  178.8 3.2 gather_fusion.1
  182.0 3.2 gather_fusion
  185.2 67.2 %all-gather.7.cloned.1.call-done = bf16[4608,4,128]{2,0,1:T(8,128)(2,1)} async-done(((bf16[72,4,128]{2,0,1:T(8,128)(2,1)}), bf16[4608,4,128]{2,0,1:T(8,128)(2,1)}) %all-gather.7.cloned.1.call-update) | async-done | bytes 4718608 | tf_op jit(solution)/shard_map/all_gather | solution.py:59
  252.5 5.2 copy.81
  260.0 109.8 %while.30 = (s32[]{:T(128)}, bf16[6,768,4]{1,2,0:T(4,128)(2,1)S(1)}, s32[12]{0:T(128)S(1)}, pred[12]{0:T(512)(128)(4,1)S(1)}, s32[12]{0:T(128)S(1)}, /*index=5*/...) while((s32[]{:T(128)}, ...), condition=%wide.region_8.10_spmd.clone, body=%wide.region_6.9_spmd.clone.sunk | while | flops 102147592 | bytes 1153013 | solution.py:111
  369.8 244.9 %pmax.7 = bf16[6,768,4]{1,2,0:T(4,128)(2,1)S(1)} all-reduce(bf16[6,768,4]{1,2,0:T(4,128)(2,1)S(1)} %get-tuple-element.418), channel_id=1, replica_groups=mesh['heads'=4,'pages'=64] {'pages'}, use_global_device_ids=true, to_apply=%region_9.11 | all-reduce | flops 18432 | bytes 73728 | tf_op jit(solution)/shard_map/pmax | solution.py:122
  614.7 4.8 broadcast_in_dim.197.clone
  619.5 196.1 %while.31 = (s32[]{:T(128)}, f32[6,768,4,128]{3,2,1,0:T(4,128)}, f32[6,768,4]{1,2,0:T(4,128)S(1)}, s32[12]{0:T(128)S(1)}, bf16[12,128,4,128]{3,1,2,0:T(8,128)(2,...) while((s32[]{:T(128)}, f32[6,768,4,128]{3,2,1,0:T(4,128)}, ...), condition=%wide.region_12.14_spmd.clone, body=%wide.region_10.13_spmd.clone.sunk | while | flops 203981312 | bytes 18659864 | solution.py:111
  627.3 2.6 fusion.53
  643.7 2.6 fusion.53
  660.0 2.6 fusion.53
  676.3 2.6 fusion.53
  692.6 2.6 fusion.53
  709.0 2.6 fusion.53
  725.3 2.6 fusion.53
  741.7 2.6 fusion.53
  758.0 2.6 fusion.53
  774.3 2.6 fusion.53
  790.7 2.6 fusion.53
  807.1 2.6 fusion.53
  816.9 8.4 copy.105
  827.3 158.9 %all-reduce.4.cloned.1.call-done = f32[4608,4]{0,1:T(4,128)} async-done(((f32[4608,4]{0,1:T(4,128)}), f32[4608,4]{0,1:T(4,128)}) %all-reduce.4.cloned.1.call-update) | async-done | bytes 73744
  987.0 77.0 %all-gather.11.cloned.1.call-done = bf16[512,4096]{0,1:T(8,128)(2,1)} async-done(((bf16[512,64]{0,1:T(8,128)(2,1)}), bf16[512,4096]{0,1:T(8,128)(2,1)}) %all-gather.11.cloned.1.call-update) | async-done | bytes 4194320 | tf_op jit(solution)/shard_map/all_gather | solution.py:169
  1064.1 156.9 %reduce-scatter.8.cloned.1.call-done = f32[72,512]{1,0:T(8,128)} async-done(((f32[4608,512]{1,0:T(8,128)}), f32[72,512]{1,0:T(8,128)}) %reduce-scatter.8.cloned.1.call-update) | async-done | bytes 147472
  1221.1 4.5 convolution_convert_fusion
  1225.6 3.9 copy.85
  1229.5 2.4 copy.86
  1231.9 17.2 %reduce-scatter.6.cloned.1.call-done = bf16[72,1024]{1,0:T(8,128)(2,1)} async-done(((bf16[72,4096]{1,0:T(8,128)(2,1)}), bf16[72,1024]{1,0:T(8,128)(2,1)}) %reduce-scatter.6.cloned.1.call-update) | async-done | bytes 147472 | tf_op jit(solution)/shard_map/reduce_scatter | solution.py:172
  (394 shorter events, 224.6 us)
Async XLA Ops:
  7.2 6.6 copy-start.9
  7.2 4.8 copy-start.4
  7.2 4.0 copy-start.5
  7.2 5.8 copy-start.7
  7.2 5.8 copy-start.8
  7.2 85.2 %all-gather.9.cloned.1.call-start = ((), (), s32[]{:S(2)}) async-start(), calls=%async_computation.4 | async-start | bytes 4792320 | tf_op jit(solution)/shard_map/all_gather | solution.py:60
  11.2 161.3 %all-gather.5.cloned.1.call-start = ((), (), s32[]{:S(2)}) async-start(), calls=%async_computation.2 | async-start | bytes 4792320 | tf_op jit(solution)/shard_map/all_gather | solution.py:61
  11.9 240.5 %all-gather.7.cloned.1.call-start = ((), (), s32[]{:S(2)}) async-start(), calls=%async_computation.3 | async-start | bytes 4792320 | tf_op jit(solution)/shard_map/all_gather | solution.py:59
  12.9 973.3 %all-reduce.4.cloned.1.call-start = ((), (), s32[]{:S(2)}) async-start(), calls=%async_computation.7 | async-start | bytes 147456
  252.5 5.2 copy-start.1
  252.5 5.2 copy-start.2
  815.6 0.6 copy-start.3
  816.3 247.8 %all-gather.11.cloned.1.call-start = ((), (), s32[]{:S(2)}) async-start(), calls=%async_computation.5 | async-start | bytes 4259840 | tf_op jit(solution)/shard_map/all_gather | solution.py:169
  816.9 404.0 %reduce-scatter.8.cloned.1.call-start = ((), (), s32[]{:S(2)}) async-start(), calls=%async_computation.8 | async-start | bytes 9584640
  825.4 0.7 copy-start.10
  825.4 423.6 %reduce-scatter.6.cloned.1.call-start = ((), (), s32[]{:S(2)}) async-start(), calls=%async_computation.6 | async-start | bytes 737280 | tf_op jit(solution)/shard_map/reduce_scatter | solution.py:172
  1225.6 3.9 copy-start
  1229.5 19.5 %copy-start.6 = (f32[1024]{0:T(1024)S(1)}, f32[1024]{0:T(1024)}, u32[]{:S(2)}) copy-start(f32[1024]{0:T(1024)} %param.25) | copy-start | bytes 12292
Sparse Core Ops, SparseCore 0:
  11.3 81.0 all-gather.8
  95.7 76.7 all-gather.4
  175.7 76.7 all-gather.6
  816.4 169.7 all-reduce.3
  988.8 75.1 all-gather.10
  1068.2 152.7 reduce-scatter.7
  1225.7 23.2 reduce-scatter.5
where the time goes:
time: 1260 us
  waiting for transfers between devices  630 us (50%)
  blocking collectives  245 us (19%)
  local copies, waits for them, and re-layouts  171 us (14%)
  matrix products  74.4 us (6%)
  loops' own time  63.8 us (5%)
  other arithmetic  58.4 us (5%)
  between operations  15 us (1%)
    unnamed x9, waiting for transfers between devices  316 us
    pmax x1, blocking collectives, per_device(): peaks = lax.pmax(peaks.astype(jnp.bfloat16), 'pages').astype(peaks.dtype)  245 us
    all_gather x1, waiting for transfers between devices, per_device(): lax.all_gather(rotated_k, 'pages', axis=0, tiled=True)  78.4 us
    all_gather x1, waiting for transfers between devices, per_device(): lax.all_gather(out_weight, 'pages', axis=1, tiled=True)  77 us
    all_gather x1, waiting for transfers between devices, per_device(): lax.all_gather(values, 'pages', axis=0, tiled=True)  73.7 us
    all_gather x1, waiting for transfers between devices, per_device(): lax.all_gather(rotated_q, 'pages', axis=0, tiled=True)  67.2 us
    another operation x2, loops' own time, over_slots(): return lax.fori_loop(0, slot_count, step, start)  63.8 us
    dot_general x24, matrix products, slot_scores(): jnp.einsum('qhd,khd->hqk', query_block, key_block, preferred_element_type...  50.4 us
  transfers between devices with their start and end apart: 7, of which 7 were waited for; matrix products, arithmetic and copies ran while one was open for 3% of the time, Pallas kernels for 0%

commit v1 on v0

--- a/solution.py
+++ b/solution.py
@@ -58,7 +58,9 @@
     all_q, all_k, all_v = (
         lax.all_gather(rotated_q, "pages", axis=0, tiled=True),
         lax.all_gather(rotated_k, "pages", axis=0, tiled=True),
-        lax.all_gather(values, "pages", axis=0, tiled=True),
+        jnp.concatenate(
+            lax.all_to_all(jnp.stack([values] * lax.axis_size("pages")), "pages", 0, 0), axis=0
+        ),
     )
     my_slots = device_at * slot_count + jnp.arange(slot_count, dtype=jnp.int32)
     cached_hit = page_table.reshape(-1)[None, :] == my_slots[:, None]

time: 1260 us -> 1210 us (0.960)
  waiting for transfers between devices: 630 us -> 566 us
    all_gather x1 -> x0, waiting for transfers between devices: 73.7 us -> none  [per_device(): lax.all_gather(values, 'pages', axis=0, tiled=True)]
    all_gather x1, waiting for transfers between devices: 67.2 us -> 41.4 us  [per_device(): lax.all_gather(rotated_q, 'pages', axis=0, tiled=True)]
    all_to_all x0 -> x1, waiting for transfers between devices: none -> 25.1 us  [per_device(): lax.all_to_all(jnp.stack([values] * lax.axis_size('pages')), 'pages', 0, 0)]
    unnamed x9 -> x8, waiting for transfers between devices: 316 us -> 317 us
where the time goes in v1:
time: 1210 us
  waiting for transfers between devices  566 us (47%)
  blocking collectives  245 us (20%)
  local copies, waits for them, and re-layouts  173 us (14%)
  matrix products  74.4 us (6%)
  loops' own time  63.8 us (5%)
  other arithmetic  57.7 us (5%)
  between operations  15 us (1%)
  starting transfers between devices  12.7 us (1%)
    unnamed x8, waiting for transfers between devices  317 us
    pmax x1, blocking collectives, per_device(): peaks = lax.pmax(peaks.astype(jnp.bfloat16), 'pages').astype(peaks.dtype)  245 us
    all_gather x1, waiting for transfers between devices, per_device(): lax.all_gather(rotated_k, 'pages', axis=0, tiled=True)  88.4 us
    all_gather x1, waiting for transfers between devices, per_device(): lax.all_gather(out_weight, 'pages', axis=1, tiled=True)  77 us
    another operation x2, loops' own time, over_slots(): return lax.fori_loop(0, slot_count, step, start)  63.8 us
    dot_general x24, matrix products, slot_scores(): jnp.einsum('qhd,khd->hqk', query_block, key_block, preferred_element_type...  50.4 us
    all_gather x1, waiting for transfers between devices, per_device(): lax.all_gather(rotated_q, 'pages', axis=0, tiled=True)  41.4 us
    and x24, other arithmetic, slot_scores(): cached_ok = is_cached[slot] & (base_pos < length)  29.8 us
  transfers between devices with their start and end apart: 7, of which 7 were waited for; matrix products, arithmetic and copies ran while one was open for 3% of the time, Pallas kernels for 0%

profile of v1, /device:TPU:8, one launch (start us, length us, event | category | flops | bytes accessed | tf_op | source)
XLA Modules:
  0.0 1207.1 jit_solution(7107225212033287395)
XLA Ops:
  11.2 2.7 stack.2
  13.9 12.4 %all-to-all-start = ((bf16[64,72,4,128]{3,1,2,0:T(8,128)(2,1)}), bf16[64,72,4,128]{3,1,2,0:T(8,128)(2,1)}, u32[]{:S(2)}, u32[]{:S(2)}) async-start(bf16[64,72,4,128]{3,1,2,0:T(8,128)(2,1)} %stack.2), calls=%async_computation | async-start | bytes 9437184 | tf_op jit(solution)/shard_map/all_to_all | solution.py:62
  28.4 88.4 %all-gather.6.cloned.1.call-done = bf16[4608,4,128]{2,0,1:T(8,128)(2,1)} async-done(((bf16[72,4,128]{2,0,1:T(8,128)(2,1)}), bf16[4608,4,128]{2,0,1:T(8,128)(2,1)}) %all-gather.6.cloned.1.call-update) | async-done | bytes 4718608 | tf_op jit(solution)/shard_map/all_gather | solution.py:60
  116.8 6.3 copy.79
  123.2 25.1 %all-to-all-done = bf16[64,72,4,128]{3,1,2,0:T(8,128)(2,1)} async-done(((bf16[64,72,4,128]{3,1,2,0:T(8,128)(2,1)}), bf16[64,72,4,128]{3,1,2,0:T(8,128)(2,1)}, u32[]{:S(2)}, u32[]{:S(2)}) %all-to-all-start) | async-done | bytes 4718624 | tf_op jit(solution)/shard_map/all_to_all | solution.py:62
  148.3 3.2 copy.72
  151.5 3.1 copy.73
  154.6 3.2 gather_fusion.1
  157.8 3.2 gather_fusion
  161.0 41.4 %all-gather.4.cloned.1.call-done = bf16[4608,4,128]{2,0,1:T(8,128)(2,1)} async-done(((bf16[72,4,128]{2,0,1:T(8,128)(2,1)}), bf16[4608,4,128]{2,0,1:T(8,128)(2,1)}) %all-gather.4.cloned.1.call-update) | async-done | bytes 4718608 | tf_op jit(solution)/shard_map/all_gather | solution.py:59
  202.4 5.2 copy.83
  209.9 110.6 %while.30 = (s32[]{:T(128)}, bf16[6,768,4]{1,2,0:T(4,128)(2,1)S(1)}, s32[12]{0:T(128)S(1)}, pred[12]{0:T(512)(128)(4,1)S(1)}, s32[12]{0:T(128)S(1)}, /*index=5*/...) while((s32[]{:T(128)}, ...), condition=%wide.region_8.10_spmd.clone, body=%wide.region_6.9_spmd.clone.sunk | while | flops 102147592 | bytes 1153013 | solution.py:113
  320.5 245.0 %pmax.7 = bf16[6,768,4]{1,2,0:T(4,128)(2,1)S(1)} all-reduce(bf16[6,768,4]{1,2,0:T(4,128)(2,1)S(1)} %get-tuple-element.418), channel_id=1, replica_groups=mesh['heads'=4,'pages'=64] {'pages'}, use_global_device_ids=true, to_apply=%region_9.11 | all-reduce | flops 18432 | bytes 73728 | tf_op jit(solution)/shard_map/pmax | solution.py:124
  565.6 4.8 broadcast_in_dim.197.clone
  570.4 194.8 %while.31 = (s32[]{:T(128)}, f32[6,768,4,128]{3,2,1,0:T(4,128)}, f32[6,768,4]{1,2,0:T(4,128)S(1)}, s32[12]{0:T(128)S(1)}, bf16[12,128,4,128]{3,1,2,0:T(8,128)(2,...) while((s32[]{:T(128)}, f32[6,768,4,128]{3,2,1,0:T(4,128)}, ...), condition=%wide.region_12.14_spmd.clone, body=%wide.region_10.13_spmd.clone.sunk | while | flops 203981312 | bytes 18659864 | solution.py:113
  578.1 2.6 fusion.53
  594.3 2.6 fusion.53
  610.5 2.6 fusion.53
  626.8 2.6 fusion.53
  659.2 2.6 fusion.53
  675.5 2.6 fusion.53
  707.9 2.6 fusion.53
  724.1 2.6 fusion.53
  740.4 2.6 fusion.53
  756.7 2.6 fusion.53
  766.5 8.4 copy.107
  776.8 159.0 %all-reduce.4.cloned.1.call-done = f32[4608,4]{0,1:T(4,128)} async-done(((f32[4608,4]{0,1:T(4,128)}), f32[4608,4]{0,1:T(4,128)}) %all-reduce.4.cloned.1.call-update) | async-done | bytes 73744
  936.7 77.0 %all-gather.8.cloned.1.call-done = bf16[512,4096]{0,1:T(8,128)(2,1)} async-done(((bf16[512,64]{0,1:T(8,128)(2,1)}), bf16[512,4096]{0,1:T(8,128)(2,1)}) %all-gather.8.cloned.1.call-update) | async-done | bytes 4194320 | tf_op jit(solution)/shard_map/all_gather | solution.py:171
  1013.7 156.9 %reduce-scatter.8.cloned.1.call-done = f32[72,512]{1,0:T(8,128)} async-done(((f32[4608,512]{1,0:T(8,128)}), f32[72,512]{1,0:T(8,128)}) %reduce-scatter.8.cloned.1.call-update) | async-done | bytes 147472
  1170.8 4.5 convolution_convert_fusion
  1175.3 3.9 copy.87
  1181.5 17.2 %reduce-scatter.6.cloned.1.call-done = bf16[72,1024]{1,0:T(8,128)(2,1)} async-done(((bf16[72,4096]{1,0:T(8,128)(2,1)}), bf16[72,1024]{1,0:T(8,128)(2,1)}) %reduce-scatter.6.cloned.1.call-update) | async-done | bytes 147472 | tf_op jit(solution)/shard_map/reduce_scatter | solution.py:174
  (395 shorter events, 231.0 us)
Async XLA Ops:
  7.2 4.0 copy-start.5
  7.2 109.7 %all-gather.6.cloned.1.call-start = ((), (), s32[]{:S(2)}) async-start(), calls=%async_computation.4 | async-start | bytes 4792320 | tf_op jit(solution)/shard_map/all_gather | solution.py:60
  13.9 12.5 %copy-start.4 = (bf16[72,4,128]{2,1,0:T(4,128)(2,1)S(1)}, bf16[72,4,128]{2,1,0:T(4,128)(2,1)}, u32[]{:S(2)}) copy-start(bf16[72,4,128]{2,1,0:T(4,128)(2,1)} %param.16) | copy-start | bytes 221188
  13.9 13.4 %copy-start.7 = (s32[6,6]{1,0:T(8,128)S(1)}, s32[6,6]{1,0:T(8,128)}, u32[]{:S(2)}) copy-start(s32[6,6]{1,0:T(8,128)} %param.23) | copy-start | bytes 436
  13.9 13.5 %copy-start.8 = (s32[6,122]{1,0:T(8,128)S(1)}, s32[6,122]{1,0:T(8,128)}, u32[]{:S(2)}) copy-start(s32[6,122]{1,0:T(8,128)} %param.22) | copy-start | bytes 8788
  13.9 14.2 %copy-start.9 = (s32[6]{0:T(128)S(1)}, s32[6]{0:T(128)}, u32[]{:S(2)}) copy-start(s32[6]{0:T(128)} %param.21) | copy-start | bytes 76
  13.9 134.4 %all-to-all-start = ((bf16[64,72,4,128]{3,1,2,0:T(8,128)(2,1)}), bf16[64,72,4,128]{3,1,2,0:T(8,128)(2,1)}, u32[]{:S(2)}, u32[]{:S(2)}) async-start(bf16[64,72,4,128]{3,1,2,0:T(8,128)(2,1)} %stack.2), calls=%async_computation | async-start | bytes 9437184 | tf_op jit(solution)/shard_map/all_to_all | solution.py:62
  26.3 176.1 %all-gather.4.cloned.1.call-start = ((), (), s32[]{:S(2)}) async-start(), calls=%async_computation.3 | async-start | bytes 4792320 | tf_op jit(solution)/shard_map/all_gather | solution.py:59
  27.3 908.5 %all-reduce.4.cloned.1.call-start = ((), (), s32[]{:S(2)}) async-start(), calls=%async_computation.7 | async-start | bytes 147456
  202.4 5.2 copy-start.1
  202.4 5.2 copy-start.2
  765.2 0.6 copy-start.3
  765.9 247.8 %all-gather.8.cloned.1.call-start = ((), (), s32[]{:S(2)}) async-start(), calls=%async_computation.5 | async-start | bytes 4259840 | tf_op jit(solution)/shard_map/all_gather | solution.py:171
  766.4 404.2 %reduce-scatter.8.cloned.1.call-start = ((), (), s32[]{:S(2)}) async-start(), calls=%async_computation.8 | async-start | bytes 9584640
  774.9 0.7 copy-start.10
  774.9 423.8 %reduce-scatter.6.cloned.1.call-start = ((), (), s32[]{:S(2)}) async-start(), calls=%async_computation.6 | async-start | bytes 737280 | tf_op jit(solution)/shard_map/reduce_scatter | solution.py:174
  1175.3 3.9 copy-start
  1179.2 19.5 %copy-start.6 = (f32[1024]{0:T(1024)S(1)}, f32[1024]{0:T(1024)}, u32[]{:S(2)}) copy-start(f32[1024]{0:T(1024)} %param.25) | copy-start | bytes 12292
Sparse Core Ops, SparseCore 0:
  11.3 105.5 all-gather.5
  120.1 82.2 all-gather.3
  766.0 169.7 all-reduce.3
  938.4 75.1 all-gather.7
  1017.8 152.7 reduce-scatter.7
  1175.4 23.2 reduce-scatter.5
